TPU v7x, 128 devices: a whole 4x4x4 slice. The times are simulated.
128 devices in a mesh: row: 8 (over z, core), col: 16 (over y, x).
Axes of the slice: x: 4, y: 4, z: 4, core: 2. Of those that a mesh axis runs over, the one named last changes fastest.
Arguments:
- singles: bfloat16 [1024, 384], P('row', 'col'), may hold values from -6 to 6
- pair_in: bfloat16 [1024, 1024, 128], P('row', 'col'), may hold values from -6 to 6
- proj_weight: bfloat16 [384, 256], P('col'), may hold values from -0.3125 to 0.3125
- gain_first: float32 [128], replicated, may hold values from 0.1 to 1.9
- first_in: bfloat16 [128, 1024], replicated, may hold values from -0.5 to 0.5
- first_out: bfloat16 [512, 128], replicated, may hold values from -0.25 to 0.25
- gain_second: float32 [128], replicated, may hold values from 0.1 to 1.9
- second_in: bfloat16 [128, 1024], replicated, may hold values from -0.5 to 0.5
- second_out: bfloat16 [512, 128], replicated, may hold values from -0.25 to 0.25
- head_weight: bfloat16 [128, 64], replicated, may hold values from -1.5 to 1.5
- pae_bins: int32 [1024, 1024], P('row', 'col'), may hold values from 0 to 63
- chain_perm: int32 [1024], replicated, may hold values from 0 to 1023, as said below
- resolved_counts: int32 [8, 16], P('row'), may hold values from 1 to 256, 2048 in all within a row
- tile_order: int32 [8, 4096], P('row', 'col'), may hold values from 0 to 255, as said below
Outputs:
- pair_grad: bfloat16 [1024, 1024, 128], P('row', 'col')
- single_grad: float32 [1024, 384], P('row', 'col')
- second_in_grad: float32 [128, 1024], replicated
- second_out_grad: float32 [512, 128], replicated
- head_grad: float32 [128, 64], replicated
Inputs may be any that keep to these rules, and one draw needn't show every extreme that they name: chain_perm maps every aligned group of 64 tokens onto itself, moving whole aligned runs of 16 tokens and keeping the order inside a run. Each row of resolved_counts sums to 2048, and its largest entry is 256. In each row of tile_order, entries b * 256 to (b + 1) * 256 - 1 are a permutation of 0 to 255.
All inputs are finite; a program needn't handle non-finite values.
Results may differ from a plain program's by a relative error of at most 0.011.
Values may be sent and summed in bfloat16 or wider, within the bound.
A program may use at most 64 MiB of HBM per device.

v0:
```python
import jax
import jax.numpy as jnp
from jax import lax
from jax.sharding import PartitionSpec as P

TILE = 32


def contract(left_op, right_op, left_dim, right_dim):
    return lax.dot_general(
        left_op,
        right_op,
        (((left_dim,), (right_dim,)), ((), ())),
        preferred_element_type=jnp.float32,
    )


def block_size(extent, per_item, limit):
    best = 1
    for candidate in range(1, extent + 1):
        if extent % candidate == 0 and candidate * per_item <= limit:
            best = candidate
    return best


def transition_forward(start_z, gain_vec, w_in, w_out):
    hidden_units = w_out.shape[0]
    average = jnp.mean(start_z, axis=-1, keepdims=True)
    centred = start_z - average
    scaling = lax.rsqrt(jnp.mean(centred * centred, axis=-1, keepdims=True) + 1e-05)
    normed = centred * scaling
    inputs = (normed * gain_vec).astype(jnp.bfloat16)
    gate_up = jnp.dot(inputs, w_in, preferred_element_type=jnp.float32)
    gate_part = gate_up[:, :hidden_units]
    up_part = gate_up[:, hidden_units:]
    gate_sig = jax.nn.sigmoid(gate_part)
    hidden_act = (gate_part * gate_sig * up_part).astype(jnp.bfloat16)
    result = jnp.dot(hidden_act, w_out, preferred_element_type=jnp.float32)
    return (result, (normed, scaling, inputs, gate_part, up_part, gate_sig, hidden_act))


def transition_backward(saved, grad_out, gain_vec, w_in, w_out, with_weights):
    normed, scaling, inputs, gate_part, up_part, gate_sig, hidden_act = saved
    grad_hidden = contract(grad_out, w_out, 1, 1)
    grad_gate = grad_hidden * up_part * gate_sig * (1.0 + gate_part * (1.0 - gate_sig))
    grad_up = grad_hidden * gate_part * gate_sig
    grad_both = jnp.concatenate([grad_gate, grad_up], axis=1).astype(jnp.bfloat16)
    grad_normed = contract(grad_both, w_in, 1, 1) * gain_vec
    grad_field = scaling * (
        grad_normed
        - jnp.mean(grad_normed, axis=-1, keepdims=True)
        - normed * jnp.mean(grad_normed * normed, axis=-1, keepdims=True)
    )
    if with_weights:
        return (grad_field, contract(inputs, grad_both, 0, 0), contract(hidden_act, grad_out, 0, 0))
    return (grad_field, None, None)


def head_step(rounded_z, targets, keep_mask, head_weight):
    logits = jnp.dot(rounded_z, head_weight, preferred_element_type=jnp.float32)
    exponent = jnp.exp(logits - jnp.max(logits, axis=-1, keepdims=True))
    probability = exponent / jnp.sum(exponent, axis=-1, keepdims=True)
    onehot = (targets[:, None] == lax.broadcasted_iota(jnp.int32, logits.shape, 1)).astype(
        jnp.float32
    )
    grad_logits = ((probability - onehot) * keep_mask[:, None]).astype(jnp.bfloat16)
    return (
        contract(grad_logits, head_weight, 1, 1).astype(jnp.bfloat16),
        contract(rounded_z, grad_logits, 0, 0),
    )


def second_step(pair_one, targets, live_mask, gain_second, second_in, second_out, head_weight):
    start_f = pair_one.astype(jnp.float32)
    delta, saved = transition_forward(start_f, gain_second, second_in, second_out)
    rounded_z = (start_f + live_mask[:, None] * delta).astype(jnp.bfloat16)
    grad_two, head_part = head_step(rounded_z, targets, jnp.ones_like(live_mask), head_weight)
    masked_out = jnp.where(live_mask[:, None] > 0, grad_two, jnp.zeros((), jnp.bfloat16))
    back_field, in_part, out_part = transition_backward(
        saved, masked_out, gain_second, second_in, second_out, True
    )
    return (
        (grad_two.astype(jnp.float32) + back_field).astype(jnp.bfloat16),
        in_part,
        out_part,
        head_part,
    )


def local(
    singles,
    pair_in,
    proj_weight,
    gain_first,
    first_in,
    first_out,
    gain_second,
    second_in,
    second_out,
    head_weight,
    pae_bins,
    chain_perm,
    resolved_counts,
    tile_order,
):
    rows_dev, cols_dev, width = pair_in.shape
    tile_len = TILE
    tiles_dev = rows_dev * cols_dev // tile_len
    token_count = chain_perm.shape[0]
    row_index = lax.axis_index("row")
    col_index = lax.axis_index("col")
    col_count = lax.axis_size("col")
    partial_proj = jnp.dot(singles, proj_weight, preferred_element_type=jnp.float32)
    projected = lax.psum(partial_proj, "col")
    left_part = projected[:, :width]
    right_part = projected[:, width:].astype(jnp.bfloat16)
    col_start = col_index * cols_dev
    right_all = lax.all_gather(right_part, "row", axis=0, tiled=True)
    col_right = lax.dynamic_slice_in_dim(right_all, col_start, cols_dev, 0)
    col_right_f = col_right.astype(jnp.float32)
    block_rows = block_size(rows_dev, cols_dev, 1024)
    row_blocks = rows_dev // block_rows
    block_pairs = block_rows * cols_dev

    def start_field(block_index):
        first_row = block_index * block_rows
        pair_rows = lax.dynamic_slice_in_dim(pair_in, first_row, block_rows, 0).astype(jnp.float32)
        left_rows = lax.dynamic_slice_in_dim(left_part, first_row, block_rows, 0)
        field_rows = pair_rows + left_rows[:, None, :] + col_right_f[None, :, :]
        return field_rows.reshape(block_pairs, width)

    def forward_block(block_index):
        start_z = start_field(block_index)
        delta, unused_saved = transition_forward(start_z, gain_first, first_in, first_out)
        return (start_z + delta).astype(jnp.bfloat16)

    block_ids = jnp.arange(row_blocks, dtype=jnp.int32)
    pair_one = lax.map(forward_block, block_ids).reshape(rows_dev * cols_dev, width)
    live_count = resolved_counts[0, col_index]
    order_list = tile_order[0]
    tile_iota = jnp.arange(tiles_dev, dtype=jnp.int32)
    rank_of = jnp.sum(
        jnp.where(order_list[None, :] == tile_iota[:, None], tile_iota[None, :], 0), axis=1
    )
    tile_live = rank_of < live_count
    pair_live = jnp.repeat(tile_live, tile_len).astype(jnp.float32)
    perm_rows = (
        lax.dynamic_slice_in_dim(chain_perm, row_index * rows_dev, rows_dev, 0)
        - row_index * rows_dev
    )
    perm_cols = lax.dynamic_slice_in_dim(chain_perm, col_start, cols_dev, 0) - col_start
    targets = jnp.take(jnp.take(pae_bins, perm_rows, axis=0), perm_cols, axis=1).reshape(
        rows_dev * cols_dev
    )
    pair_stack = pair_one.reshape(row_blocks, block_pairs, width)
    target_stack = targets.reshape(row_blocks, block_pairs)
    live_stack = pair_live.reshape(row_blocks, block_pairs)
    zero_in = jnp.zeros(second_in.shape, jnp.float32)
    zero_out = jnp.zeros(second_out.shape, jnp.float32)
    zero_head = jnp.zeros(head_weight.shape, jnp.float32)

    def head_block(running, operands):
        grad_two, head_part = head_step(operands[0], operands[1], 1.0 - operands[2], head_weight)
        return (running + head_part, grad_two)

    head_sum, rest_stack = lax.scan(head_block, zero_head, (pair_stack, target_stack, live_stack))
    rest_tiles = rest_stack.reshape(tiles_dev, tile_len, width)
    slots = -(-tiles_dev // col_count)
    row_counts = resolved_counts[0]
    offsets = jnp.cumsum(row_counts) - row_counts
    my_offset = offsets[col_index]
    worker_iota = jnp.arange(col_count, dtype=jnp.int32)[:, None]
    slot_iota = jnp.arange(slots, dtype=jnp.int32)[None, :]
    send_rank = col_count * slot_iota + jnp.mod(worker_iota - my_offset, col_count)
    send_valid = send_rank < live_count
    send_ids = order_list[jnp.minimum(send_rank, tiles_dev - 1)]
    tile_view = pair_one.reshape(tiles_dev, tile_len, width)
    target_view = targets.reshape(tiles_dev, tile_len).astype(jnp.bfloat16)
    send_pairs = jnp.where(
        send_valid[:, :, None, None], tile_view[send_ids], jnp.zeros((), jnp.bfloat16)
    )
    send_targets = jnp.where(
        send_valid[:, :, None], target_view[send_ids], jnp.zeros((), jnp.bfloat16)
    )
    recv_pairs, recv_targets = (
        lax.all_to_all(send_pairs, "col", split_axis=0, concat_axis=0, tiled=True),
        lax.all_to_all(send_targets, "col", split_axis=0, concat_axis=0, tiled=True),
    )
    work_count = tiles_dev // 2
    position = jnp.arange(work_count, dtype=jnp.int32)
    global_rank = col_count * position + col_index
    source = jnp.sum((offsets[None, :] <= global_rank[:, None]).astype(jnp.int32), axis=1) - 1
    source_slot = (global_rank - offsets[source]) // col_count
    flat_index = source * slots + source_slot
    work_pairs = recv_pairs.reshape(col_count * slots, tile_len, width)[flat_index]
    work_targets = recv_targets.reshape(col_count * slots, tile_len)[flat_index].astype(jnp.int32)
    block_tiles = block_size(work_count, tile_len, 1024)
    work_blocks = work_count // block_tiles
    work_pair_stack = work_pairs.reshape(work_blocks, block_tiles * tile_len, width)
    work_target_stack = work_targets.reshape(work_blocks, block_tiles * tile_len)

    def worker_block(running, operands):
        all_live = jnp.ones(operands[1].shape, jnp.float32)
        grad_one, in_part, out_part, head_part = second_step(
            operands[0], operands[1], all_live, gain_second, second_in, second_out, head_weight
        )
        return ((running[0] + in_part, running[1] + out_part, running[2] + head_part), grad_one)

    weight_sums, work_grad_stack = lax.scan(
        worker_block, (zero_in, zero_out, head_sum), (work_pair_stack, work_target_stack)
    )
    work_grads = work_grad_stack.reshape(work_count, tile_len, width)
    back_rank = col_count * slot_iota + jnp.mod(col_index - offsets[:, None], col_count)
    back_valid = back_rank < row_counts[:, None]
    back_position = jnp.minimum((offsets[:, None] + back_rank) // col_count, work_count - 1)
    back_pairs = jnp.where(
        back_valid[:, :, None, None], work_grads[back_position], jnp.zeros((), jnp.bfloat16)
    )
    returned = lax.all_to_all(back_pairs, "col", split_axis=0, concat_axis=0, tiled=True)
    tile_worker = jnp.mod(my_offset + rank_of, col_count)
    tile_slot = jnp.minimum(rank_of // col_count, slots - 1)
    from_worker = returned.reshape(col_count * slots, tile_len, width)[
        tile_worker * slots + tile_slot
    ]
    grad_one_all = jnp.where(tile_live[:, None, None], from_worker, rest_tiles).reshape(
        rows_dev * cols_dev, width
    )
    grad_one_stack = grad_one_all.reshape(row_blocks, block_pairs, width)

    def backward_block(running, operands):
        block_index, grad_one = operands
        start_z = start_field(block_index)
        unused_delta, saved = transition_forward(start_z, gain_first, first_in, first_out)
        back_field, unused_in, unused_out = transition_backward(
            saved, grad_one, gain_first, first_in, first_out, False
        )
        grad_zero = (grad_one.astype(jnp.float32) + back_field).reshape(block_rows, cols_dev, width)
        return (
            running + jnp.sum(grad_zero, axis=0),
            (grad_zero.astype(jnp.bfloat16), jnp.sum(grad_zero, axis=1)),
        )

    right_grad, (pair_grad_stack, left_stack) = lax.scan(
        backward_block, jnp.zeros((cols_dev, width), jnp.float32), (block_ids, grad_one_stack)
    )
    pair_grad = pair_grad_stack.reshape(rows_dev, cols_dev, width)
    left_grad = left_stack.reshape(rows_dev, width)
    token_part = jnp.zeros((token_count, 2 * width), jnp.float32)
    token_part = lax.dynamic_update_slice(token_part, left_grad, (row_index * rows_dev, 0))
    token_part = lax.dynamic_update_slice(token_part, right_grad, (col_start, width))
    token_total, in_total, out_total, head_total = lax.psum(
        (token_part, weight_sums[0], weight_sums[1], weight_sums[2]), ("row", "col")
    )
    token_rows = lax.dynamic_slice_in_dim(token_total, row_index * rows_dev, rows_dev, 0).astype(
        jnp.bfloat16
    )
    single_grad = contract(token_rows, proj_weight, 1, 1)
    return (
        pair_grad,
        single_grad,
        in_total / token_count,
        out_total / token_count,
        head_total / token_count,
    )


def solution(mesh):
    in_specs = (
        P("row", "col"),
        P("row", "col", None),
        P("col", None),
        P(),
        P(),
        P(),
        P(),
        P(),
        P(),
        P(),
        P("row", "col"),
        P(),
        P("row", None),
        P("row", "col"),
    )
    out_specs = (P("row", "col", None), P("row", "col"), P(), P(), P())
    return jax.shard_map(local, mesh=mesh, in_specs=in_specs, out_specs=out_specs, check_vma=False)
```

profile of v0, /device:TPU:1, one launch (start us, length us, event | category | flops | bytes accessed | tf_op | source)
XLA Modules:
  0.0 618.8 jit_solution(7770418198475508663)
XLA Ops:
  21.9 7.6 %all-to-all-start.1 = ((bf16[16,2,256]{2,1,0:T(2,128)(2,1)}), bf16[16,2,256]{2,1,0:T(2,128)(2,1)S(1)}, u32[]{:S(2)}, u32[]{:S(2)}) async-start(bf16[16,2,256]{2,1,0:T(2,128)(2,1)} %reshape.938), calls=%async_computation.1 | async-start | bytes 32768 | tf_op jit(solution)/shard_map/all_to_all | solution.py:187
  30.6 10.0 %fusion.77 = s32[128]{0:T(128)S(1)} fusion(s32[128]{0:T(128)S(1)} %convert_reduce_fusion.1, s32[]{:T(128)} %bitcast.33, s32[]{:T(128)} %bitcast.34, s32[]{:T(128)} %bitcast.35, s32[]{:T(128)} %bitcast.36, s32[]{:T(128)} %bitcast.37, s32[]{:T(128)} %bitcast.39, s32[]{:T(128)} %bitcast.38, s32[]{:T(128)} %bitcast.16, s32[]{:T(128)} %bitcast.18, s32[]{:T(128)} %bitcast.20, ...), kind=kLoop, calls=%fused_computation.208 | loop fusion | flops 7296 | bytes 1092 | tf_op jit(solution)/shard_map/select_n | solution.py:195
  42.0 54.0 %all-reduce.6.cloned.1.call-done = f32[128,256]{1,0:T(8,128)} async-done(((f32[128,256]{1,0:T(8,128)}), f32[128,256]{1,0:T(8,128)}) %all-reduce.6.cloned.1.call-update) | async-done | bytes 131088 | tf_op jit(solution)/shard_map/psum | solution.py:114
  96.8 15.6 %all_gather.3 = bf16[1024,128]{1,0:T(8,128)(2,1)S(1)} all-gather(bf16[128,128]{1,0:T(8,128)(2,1)S(1)} %slice.95), channel_id=1, replica_groups=mesh['row'=8,'col'=16] {'row'}, dimensions={0}, use_global_device_ids=true | all-gather | bytes 294912 | tf_op jit(solution)/shard_map/all_gather | solution.py:118
  115.5 64.0 %while.55 = (s32[]{:T(128)}, bf16[8,1024,128]{2,1,0:T(8,128)(2,1)}, s32[8]{0:T(128)S(1)}, bf16[128,64,128]{2,1,0:T(8,128)(2,1)}, f32[128,128]{1,0:T(8,128)}, /*i...) while((s32[]{:T(128)}, bf16[8,1024,128]{2,1,0:T(8,128)(2,1)}, ...), condition=%wide.region_6.7_spmd, body=%wide.region_3.6_spmd.sunk | while | flops 407897088 | bytes 11818179 | solution.py:138
  121.2 2.3 fusion.163
  129.2 2.3 fusion.163
  137.2 2.3 fusion.163
  145.2 2.3 fusion.163
  153.2 2.3 fusion.163
  161.2 2.3 fusion.163
  169.2 2.3 fusion.163
  177.2 2.3 fusion.163
  179.6 2.6 gather_fusion.3
  183.7 4.8 all-to-all-start
  189.2 22.2 %while.56 = (s32[]{:T(128)}, f32[128,64]{0,1:T(8,128)S(1)}, bf16[8,1024,128]{2,1,0:T(8,128)(2,1)S(1)}, bf16[8,1024,128]{2,1,0:T(8,128)(2,1)}, bf16[128,64]{0,1:T...) while((s32[]{:T(128)}, f32[128,64]{0,1:T(8,128)S(1)}, ...), condition=%wide.region_10.11_spmd.clone, body=%wide.region_7.10_spmd.clone.sunk | while | flops 51592192 | bytes 1995891 | solution.py:166
  211.5 9.9 %all-to-all-done = bf16[16,16,32,128]{3,2,1,0:T(8,128)(2,1)} async-done(((bf16[16,16,32,128]{3,2,1,0:T(8,128)(2,1)}), bf16[16,16,32,128]{3,2,1,0:T(8,128)(2,1)}, u32[]{:S(2)}, u32[]{:S(2)}) %all-to-all-start) | async-done | bytes 2097184 | tf_op jit(solution)/shard_map/all_to_all | solution.py:186
  221.4 2.4 gather_fusion.4
  223.8 45.5 %while.57 = (s32[]{:T(128)}, f32[128,1024]{1,0:T(8,128)}, f32[512,128]{1,0:T(8,128)S(1)}, f32[128,64]{0,1:T(8,128)S(1)}, bf16[4,1024,128]{2,1,0:T(8,128)(2,1)}, ...) while((s32[]{:T(128)}, f32[128,1024]{1,0:T(8,128)}, ...), condition=%wide.region_19.20_spmd.clone, body=%wide.region_12.19_spmd.clone.sunk | while | flops 1282874368 | bytes 39037144 | solution.py:209
  231.5 3.5 fusion.189
  242.8 3.7 fusion.189
  254.2 3.7 fusion.189
  265.6 3.7 fusion.189
  269.3 2.3 gather_fusion.7
  273.2 3.7 all-to-all-start.2
  278.3 161.1 %all-reduce.8.cloned.1.call-done = (f32[128,1024]{1,0:T(8,128)}, f32[512,128]{1,0:T(8,128)}) async-done(((f32[128,1024]{1,0:T(8,128)}, f32[512,128]{1,0:T(8,128)}), (f32[128,1024]{1,0:T(8,128)}, f32[512,128]{1,0:T(8,128)})) %all-reduce.8.cloned.1.call-update) | async-done | bytes 786448 | tf_op jit(solution)/shard_map/psum | solution.py:251
  443.0 2.2 gather_fusion.8
  445.2 3.6 bitcast_select_fusion
  448.7 89.8 %while.58 = (s32[]{:T(128)}, f32[64,128]{1,0:T(8,128)S(1)}, bf16[8,16,64,128]{3,2,1,0:T(8,128)(2,1)}, f32[8,16,128]{2,1,0:T(8,128)}, bf16[8,1024,128]{2,1,0:T(8,...) while((s32[]{:T(128)}, f32[64,128]{1,0:T(8,128)S(1)}, ...), condition=%wide.region_27.28_spmd.clone, body=%wide.region_20.27_spmd.clone.sunk | while | flops 686169088 | bytes 20674808 | solution.py:243
  488.2 2.0 fusion.198
  533.0 2.0 fusion.198
  539.5 71.1 %all-reduce.9 = (bf16[1024,256]{1,0:T(8,128)(2,1)S(1)}, f32[128,64]{0,1:T(8,128)S(1)}) all-reduce(f32[1024,256]{1,0:T(8,128)S(1)} %constant_dynamic-update-slice_fusion.2, f32[128,64]{0,1:T(8,128)S(1)} %get-tuple-element.223), channel_id=1, replica_groups=mesh['row'=8,'col'=16] {'row','col'}, use_global_device_ids=true, to_apply=%region_28.29 | all-reduce | flops 270336 | bytes 1638400 | tf_op jit(solution)/shard_map/psum | solution.py:251
  (472 shorter events, 203.6 us)
Async XLA Ops:
  7.2 0.7 copy-start
  7.2 6.6 %copy-start.1 = (s32[1,256]{1,0:T(1,128)S(1)}, s32[1,256]{1,0:T(1,128)}, u32[]{:S(2)}) copy-start(s32[1,256]{1,0:T(1,128)} %param.35) | copy-start | bytes 3076
  7.2 88.8 %all-reduce.6.cloned.1.call-start = ((), (), s32[]{:S(2)}) async-start(), calls=%async_computation.3 | async-start | bytes 262144 | tf_op jit(solution)/shard_map/psum | solution.py:114
  13.8 3.7 copy-start.9
  13.8 5.6 copy-start.11
  20.2 95.3 %copy-start.2 = (bf16[128,1024]{1,0:T(8,128)(2,1)S(1)}, bf16[128,1024]{1,0:T(8,128)(2,1)}, u32[]{:S(2)}) copy-start(bf16[128,1024]{1,0:T(8,128)(2,1)} %param.26) | copy-start | bytes 786436
  20.2 95.3 %copy-start.8 = (f32[128]{0:T(128)S(1)}, f32[128]{0:T(128)}, u32[]{:S(2)}) copy-start(f32[128]{0:T(128)} %param.25) | copy-start | bytes 1540
  21.9 19.1 %all-to-all-start.1 = ((bf16[16,2,256]{2,1,0:T(2,128)(2,1)}), bf16[16,2,256]{2,1,0:T(2,128)(2,1)S(1)}, u32[]{:S(2)}, u32[]{:S(2)}) async-start(bf16[16,2,256]{2,1,0:T(2,128)(2,1)} %reshape.938), calls=%async_computation.1 | async-start | bytes 32768 | tf_op jit(solution)/shard_map/all_to_all | solution.py:187
  183.7 37.7 %all-to-all-start = ((bf16[16,16,32,128]{3,2,1,0:T(8,128)(2,1)}), bf16[16,16,32,128]{3,2,1,0:T(8,128)(2,1)}, u32[]{:S(2)}, u32[]{:S(2)}) async-start(bf16[16,16,32,128]{3,2,1,0:T(8,128)(2,1)} %broadcast_select_fusion), calls=%async_computation | async-start | bytes 4194304 | tf_op jit(solution)/shard_map/all_to_all | solution.py:186
  188.5 0.7 copy-start.7
  211.4 10.0 %copy-start.4 = (bf16[8,1024,128]{2,1,0:T(8,128)(2,1)}, bf16[8,1024,128]{2,1,0:T(8,128)(2,1)S(1)}, u32[]{:S(2)}) copy-start(bf16[8,1024,128]{2,1,0:T(8,128)(2,1)S(1)} %get-tuple-element.217) | copy-start | bytes 6291460
  211.4 12.3 %copy-start.5 = (bf16[128,1024]{1,0:T(8,128)(2,1)S(1)}, bf16[128,1024]{1,0:T(8,128)(2,1)}, u32[]{:S(2)}) copy-start(bf16[128,1024]{1,0:T(8,128)(2,1)} %param.29) | copy-start | bytes 786436
  211.4 12.3 %copy-start.6 = (bf16[512,128]{1,0:T(8,128)(2,1)S(1)}, bf16[512,128]{1,0:T(8,128)(2,1)}, u32[]{:S(2)}) copy-start(bf16[512,128]{1,0:T(8,128)(2,1)} %param.30) | copy-start | bytes 393220
  211.4 12.3 %copy-start.10 = (f32[128]{0:T(128)S(1)}, f32[128]{0:T(128)}, u32[]{:S(2)}) copy-start(f32[128]{0:T(128)} %param.28) | copy-start | bytes 1540
  228.1 1.4 copy-start.12
  228.1 1.4 copy-start.13
  239.4 1.4 copy-start.12
  239.4 1.4 copy-start.13
  250.8 1.4 copy-start.12
  250.8 1.4 copy-start.13
  262.2 1.4 copy-start.12
  262.2 1.4 copy-start.13
  269.3 2.3 copy-start.3
  273.2 169.8 %all-to-all-start.2 = ((bf16[16,16,32,128]{3,2,1,0:T(8,128)(2,1)}), bf16[16,16,32,128]{3,2,1,0:T(8,128)(2,1)S(1)}, u32[]{:S(2)}, u32[]{:S(2)}) async-start(bf16[16,16,32,128]{3,2,1,0:T(8,128)(2,1)} %broadcast_select_fusion.1), calls=%async_computation.2 | async-start | bytes 4194304 | tf_op jit(solution)/shard_map/all_to_all | solution.py:219
  276.9 162.6 %all-reduce.8.cloned.1.call-start = ((), (), s32[]{:S(2)}) async-start(), calls=%async_computation.4 | async-start | bytes 1572864 | tf_op jit(solution)/shard_map/psum | solution.py:251
Sparse Core Ops, SparseCore 0:
  11.8 84.1 all-reduce.5
  283.0 156.3 all-reduce.7
where the time goes:
time: 623 us; the launch traced here: 619 us
  waiting for transfers between devices  226 us (36%)
  matrix products  115 us (18%)
  other arithmetic  88.6 us (14%)
  blocking collectives  86.8 us (14%)
  local copies, waits for them, and re-layouts  58.9 us (9%)
  starting transfers between devices  16.4 us (3%)
  between operations  14.5 us (2%)
  loops' own time  12.6 us (2%)
    psum x1, waiting for transfers between devices, local(): lax.psum((token_part, weight_sums[0], weight_sums[1], weight_sums[2]), ('...  161 us
    psum x1, blocking collectives, local(): lax.psum((token_part, weight_sums[0], weight_sums[1], weight_sums[2]), ('...  71.1 us
    dot_general x57, matrix products, contract(): lax.dot_general(left_op, right_op, (((left_dim,), (right_dim,)), ((), ())...  68 us
    psum x1, waiting for transfers between devices, local(): projected = lax.psum(partial_proj, 'col')  54 us
    reduce_sum x20, other arithmetic, transition_forward(): jnp.mean(centred * centred, axis=-1, keepdims=True) + 1e-05  23.1 us
    dot_general x12, matrix products, transition_forward(): result = jnp.dot(hidden_act, w_out, preferred_element_type=jnp.float32)  20.6 us
    reduce_sum x20, other arithmetic, transition_forward(): average = jnp.mean(start_z, axis=-1, keepdims=True)  19.2 us
    all_gather x1, blocking collectives, local(): right_all = lax.all_gather(right_part, 'row', axis=0, tiled=True)  15.6 us
  transfers between devices with their start and end apart: 5, of which 3 were waited for; matrix products, arithmetic and copies ran while one was open for 8% of the time, Pallas kernels for 0%

commit v1 on v0

--- a/solution.py
+++ b/solution.py
@@ -4,6 +4,12 @@
 from jax.sharding import PartitionSpec as P
 
 TILE = 32
+
+
+def summed_here(x, axis):
+    parts = lax.all_gather(x, axis, axis=0, tiled=False)
+    summed = parts.sum(axis=0)
+    return summed
 
 
 def contract(left_op, right_op, left_dim, right_dim):
@@ -111,7 +117,7 @@
     col_index = lax.axis_index("col")
     col_count = lax.axis_size("col")
     partial_proj = jnp.dot(singles, proj_weight, preferred_element_type=jnp.float32)
-    projected = lax.psum(partial_proj, "col")
+    projected = summed_here(partial_proj, "col")
     left_part = projected[:, :width]
     right_part = projected[:, width:].astype(jnp.bfloat16)
     col_start = col_index * cols_dev

time: 623 us -> 568 us (0.912)
  waiting for transfers between devices: 226 us -> 187 us
  local copies, waits for them, and re-layouts: 58.9 us -> 39.9 us
  other arithmetic: 88.6 us -> 99.8 us
  matrix products: 115 us -> 108 us
    psum x1 -> x0, waiting for transfers between devices: 54 us -> none  [local(): projected = lax.psum(partial_proj, 'col')]
    all_gather x0 -> x1, waiting for transfers between devices: none -> 15.2 us  [summed_here(): parts = lax.all_gather(x, axis, axis=0, tiled=False)]
    dynamic_slice x16, local copies, waits for them, and re-layouts: 11.3 us -> 0.13 us  [start_field(): left_rows = lax.dynamic_slice_in_dim(left_part, first_row, block_rows, 0)]
    reduce_sum x8, other arithmetic: 4.99 us -> 12.8 us  [backward_block(): jnp.sum(grad_zero, axis=1)]
    dot_general x12, matrix products: 20.6 us -> 13.3 us  [transition_forward(): result = jnp.dot(hidden_act, w_out, preferred_element_type=jnp.float32)]
  transfers between devices with their start and end apart: 5 -> 5, of which waited for: 3 -> 3; matrix products, arithmetic and copies ran while one was open for 8% -> 9% of each run, Pallas kernels for 0% -> 0%
where the time goes in v1:
time: 568 us; the launch traced here: 565 us
  waiting for transfers between devices  187 us (33%)
  matrix products  108 us (19%)
  other arithmetic  99.8 us (18%)
  blocking collectives  86.5 us (15%)
  local copies, waits for them, and re-layouts  39.9 us (7%)
  starting transfers between devices  16.3 us (3%)
  between operations  14.5 us (3%)
  loops' own time  12.7 us (2%)
    psum x1, waiting for transfers between devices, local(): lax.psum((token_part, weight_sums[0], weight_sums[1], weight_sums[2]), ('...  161 us
    psum x1, blocking collectives, local(): lax.psum((token_part, weight_sums[0], weight_sums[1], weight_sums[2]), ('...  71.1 us
    dot_general x57, matrix products, contract(): lax.dot_general(left_op, right_op, (((left_dim,), (right_dim,)), ((), ())...  68.3 us
    reduce_sum x20, other arithmetic, transition_forward(): jnp.mean(centred * centred, axis=-1, keepdims=True) + 1e-05  23.1 us
    reduce_sum x20, other arithmetic, transition_forward(): average = jnp.mean(start_z, axis=-1, keepdims=True)  19.3 us
    all_gather x1, blocking collectives, local(): right_all = lax.all_gather(right_part, 'row', axis=0, tiled=True)  15.4 us
    all_gather x1, waiting for transfers between devices, summed_here(): parts = lax.all_gather(x, axis, axis=0, tiled=False)  15.2 us
    dot_general x20, matrix products, transition_forward(): gate_up = jnp.dot(inputs, w_in, preferred_element_type=jnp.float32)  15.1 us
  transfers between devices with their start and end apart: 5, of which 3 were waited for; matrix products, arithmetic and copies ran while one was open for 9% of the time, Pallas kernels for 0%

profile of v1, /device:TPU:1, one launch (start us, length us, event | category | flops | bytes accessed | tf_op | source)
XLA Modules:
  0.0 565.0 jit_solution(3548427550902303094)
XLA Ops:
  13.9 1.9 gather_fusion.2
  21.9 7.6 %all-to-all-start.1 = ((bf16[16,2,256]{2,1,0:T(2,128)(2,1)}), bf16[16,2,256]{2,1,0:T(2,128)(2,1)S(1)}, u32[]{:S(2)}, u32[]{:S(2)}) async-start(bf16[16,2,256]{2,1,0:T(2,128)(2,1)} %reshape.939), calls=%async_computation.1 | async-start | bytes 32768 | tf_op jit(solution)/shard_map/all_to_all | solution.py:193
  29.9 10.0 %fusion.77 = s32[128]{0:T(128)S(1)} fusion(s32[128]{0:T(128)S(1)} %convert_reduce_fusion.1, s32[]{:T(128)} %bitcast.34, s32[]{:T(128)} %bitcast.35, s32[]{:T(128)} %bitcast.36, s32[]{:T(128)} %bitcast.37, s32[]{:T(128)} %bitcast.38, s32[]{:T(128)} %bitcast.40, s32[]{:T(128)} %bitcast.39, s32[]{:T(128)} %bitcast.17, s32[]{:T(128)} %bitcast.19, s32[]{:T(128)} %bitcast.21, ...), kind=kLoop, calls=%fused_computation.208 | loop fusion | flops 7296 | bytes 1092 | tf_op jit(solution)/shard_map/select_n | solution.py:201
  42.0 15.2 %all-gather.3.cloned.1.call-done = f32[2048,256]{1,0:T(8,128)} async-done(((f32[128,256]{1,0:T(8,128)}), f32[2048,256]{1,0:T(8,128)}) %all-gather.3.cloned.1.call-update) | async-done | bytes 2097168 | tf_op jit(solution)/shard_map/all_gather | solution.py:10
  59.1 15.4 %all_gather.11 = bf16[1024,128]{1,0:T(8,128)(2,1)S(1)} all-gather(bf16[128,128]{1,0:T(8,128)(2,1)S(1)} %slice.95), channel_id=1, replica_groups=mesh['row'=8,'col'=16] {'row'}, dimensions={0}, use_global_device_ids=true | all-gather | bytes 294912 | tf_op jit(solution)/shard_map/all_gather | solution.py:124
  76.0 51.3 %while.55 = (s32[]{:T(128)}, bf16[8,1024,128]{2,1,0:T(8,128)(2,1)}, s32[8]{0:T(128)S(1)}, bf16[128,64,128]{2,1,0:T(8,128)(2,1)}, f32[128,128]{1,0:T(8,128)S(1)},...) while((s32[]{:T(128)}, bf16[8,1024,128]{2,1,0:T(8,128)(2,1)}, ...), condition=%wide.region_6.7_spmd, body=%wide.region_3.6_spmd.sunk | while | flops 407897088 | bytes 11818179 | solution.py:144
  127.4 2.6 gather_fusion.3
  131.5 4.7 all-to-all-start
  137.0 22.1 %while.56 = (s32[]{:T(128)}, f32[128,64]{0,1:T(8,128)S(1)}, bf16[8,1024,128]{2,1,0:T(8,128)(2,1)S(1)}, bf16[8,1024,128]{2,1,0:T(8,128)(2,1)}, bf16[128,64]{0,1:T...) while((s32[]{:T(128)}, f32[128,64]{0,1:T(8,128)S(1)}, ...), condition=%wide.region_10.11_spmd.clone, body=%wide.region_7.10_spmd.clone.sunk | while | flops 51592192 | bytes 1995891 | solution.py:172
  159.2 10.0 %all-to-all-done = bf16[16,16,32,128]{3,2,1,0:T(8,128)(2,1)} async-done(((bf16[16,16,32,128]{3,2,1,0:T(8,128)(2,1)}), bf16[16,16,32,128]{3,2,1,0:T(8,128)(2,1)}, u32[]{:S(2)}, u32[]{:S(2)}) %all-to-all-start) | async-done | bytes 2097184 | tf_op jit(solution)/shard_map/all_to_all | solution.py:192
  169.1 2.4 gather_fusion.4
  171.5 45.5 %while.57 = (s32[]{:T(128)}, f32[128,1024]{1,0:T(8,128)}, f32[512,128]{1,0:T(8,128)S(1)}, f32[128,64]{0,1:T(8,128)S(1)}, bf16[4,1024,128]{2,1,0:T(8,128)(2,1)}, ...) while((s32[]{:T(128)}, f32[128,1024]{1,0:T(8,128)}, ...), condition=%wide.region_19.20_spmd.clone, body=%wide.region_12.19_spmd.clone.sunk | while | flops 1282874368 | bytes 39037144 | solution.py:215
  179.3 3.5 fusion.189
  190.6 3.7 fusion.189
  202.0 3.7 fusion.189
  213.4 3.7 fusion.189
  217.1 2.3 gather_fusion.7
  220.9 3.7 all-to-all-start.2
  226.2 161.1 %all-reduce.5.cloned.1.call-done = (f32[128,1024]{1,0:T(8,128)}, f32[512,128]{1,0:T(8,128)}) async-done(((f32[128,1024]{1,0:T(8,128)}, f32[512,128]{1,0:T(8,128)}), (f32[128,1024]{1,0:T(8,128)}, f32[512,128]{1,0:T(8,128)})) %all-reduce.5.cloned.1.call-update) | async-done | bytes 786448 | tf_op jit(solution)/shard_map/psum | solution.py:257
  388.9 1.9 broadcast_multiply_fusion.7
  390.8 2.2 gather_fusion.8
  392.9 4.8 bitcast_select_fusion
  397.8 87.8 %while.58 = (s32[]{:T(128)}, f32[64,128]{1,0:T(8,128)S(1)}, bf16[8,16,64,128]{3,2,1,0:T(8,128)(2,1)}, f32[8,16,128]{2,1,0:T(8,128)S(1)}, bf16[8,1024,128]{2,1,0:...) while((s32[]{:T(128)}, f32[64,128]{1,0:T(8,128)S(1)}, ...), condition=%wide.region_27.28_spmd.clone, body=%wide.region_20.27_spmd.clone.sunk | while | flops 686169088 | bytes 20674808 | solution.py:249
  402.8 2.1 fusion.198
  413.8 2.1 fusion.198
  424.8 2.1 fusion.198
  435.7 2.1 fusion.198
  446.7 2.1 fusion.198
  457.7 2.1 fusion.198
  468.7 2.1 fusion.198
  479.6 2.1 fusion.198
  485.7 71.1 %all-reduce.6 = (bf16[1024,256]{1,0:T(8,128)(2,1)S(1)}, f32[128,64]{0,1:T(8,128)S(1)}) all-reduce(f32[1024,256]{1,0:T(8,128)S(1)} %constant_dynamic-update-slice_fusion.2, f32[128,64]{0,1:T(8,128)S(1)} %get-tuple-element.223), channel_id=1, replica_groups=mesh['row'=8,'col'=16] {'row','col'}, use_global_device_ids=true, to_apply=%region_28.29 | all-reduce | flops 270336 | bytes 1638400 | tf_op jit(solution)/shard_map/psum | solution.py:257
  (477 shorter events, 189.7 us)
Async XLA Ops:
  7.2 0.7 copy-start
  7.2 6.7 %copy-start.1 = (s32[1,256]{1,0:T(1,128)S(1)}, s32[1,256]{1,0:T(1,128)}, u32[]{:S(2)}) copy-start(s32[1,256]{1,0:T(1,128)} %param.35) | copy-start | bytes 3076
  7.2 50.1 %all-gather.3.cloned.1.call-start = ((), (), s32[]{:S(2)}) async-start(), calls=%async_computation.3 | async-start | bytes 2228224 | tf_op jit(solution)/shard_map/all_gather | solution.py:10
  13.8 2.1 copy-start.9
  15.8 4.6 copy-start.11
  21.9 19.1 %all-to-all-start.1 = ((bf16[16,2,256]{2,1,0:T(2,128)(2,1)}), bf16[16,2,256]{2,1,0:T(2,128)(2,1)S(1)}, u32[]{:S(2)}, u32[]{:S(2)}) async-start(bf16[16,2,256]{2,1,0:T(2,128)(2,1)} %reshape.939), calls=%async_computation.1 | async-start | bytes 32768 | tf_op jit(solution)/shard_map/all_to_all | solution.py:193
  57.2 18.8 %copy-start.2 = (bf16[128,1024]{1,0:T(8,128)(2,1)S(1)}, bf16[128,1024]{1,0:T(8,128)(2,1)}, u32[]{:S(2)}) copy-start(bf16[128,1024]{1,0:T(8,128)(2,1)} %param.26) | copy-start | bytes 786436
  57.2 18.8 %copy-start.8 = (f32[128]{0:T(128)S(1)}, f32[128]{0:T(128)}, u32[]{:S(2)}) copy-start(f32[128]{0:T(128)} %param.25) | copy-start | bytes 1540
  57.3 18.8 %copy-start.12 = (bf16[512,128]{1,0:T(8,128)(2,1)S(1)}, bf16[512,128]{1,0:T(8,128)(2,1)}, u32[]{:S(2)}) copy-start(bf16[512,128]{1,0:T(8,128)(2,1)} %param.27) | copy-start | bytes 393220
  131.5 37.6 %all-to-all-start = ((bf16[16,16,32,128]{3,2,1,0:T(8,128)(2,1)}), bf16[16,16,32,128]{3,2,1,0:T(8,128)(2,1)}, u32[]{:S(2)}, u32[]{:S(2)}) async-start(bf16[16,16,32,128]{3,2,1,0:T(8,128)(2,1)} %broadcast_select_fusion), calls=%async_computation | async-start | bytes 4194304 | tf_op jit(solution)/shard_map/all_to_all | solution.py:192
  136.3 0.7 copy-start.7
  159.1 10.0 %copy-start.4 = (bf16[8,1024,128]{2,1,0:T(8,128)(2,1)}, bf16[8,1024,128]{2,1,0:T(8,128)(2,1)S(1)}, u32[]{:S(2)}) copy-start(bf16[8,1024,128]{2,1,0:T(8,128)(2,1)S(1)} %get-tuple-element.217) | copy-start | bytes 6291460
  159.1 12.4 %copy-start.5 = (bf16[128,1024]{1,0:T(8,128)(2,1)S(1)}, bf16[128,1024]{1,0:T(8,128)(2,1)}, u32[]{:S(2)}) copy-start(bf16[128,1024]{1,0:T(8,128)(2,1)} %param.29) | copy-start | bytes 786436
  159.2 12.4 %copy-start.6 = (bf16[512,128]{1,0:T(8,128)(2,1)S(1)}, bf16[512,128]{1,0:T(8,128)(2,1)}, u32[]{:S(2)}) copy-start(bf16[512,128]{1,0:T(8,128)(2,1)} %param.30) | copy-start | bytes 393220
  159.2 12.4 %copy-start.10 = (f32[128]{0:T(128)S(1)}, f32[128]{0:T(128)}, u32[]{:S(2)}) copy-start(f32[128]{0:T(128)} %param.28) | copy-start | bytes 1540
  175.9 1.4 copy-start.14
  175.9 1.4 copy-start.15
  187.1 1.4 copy-start.14
  187.2 1.4 copy-start.15
  198.6 1.4 copy-start.14
  198.6 1.4 copy-start.15
  210.0 1.4 copy-start.14
  210.0 1.4 copy-start.15
  217.1 2.3 copy-start.3
  220.9 169.8 %all-to-all-start.2 = ((bf16[16,16,32,128]{3,2,1,0:T(8,128)(2,1)}), bf16[16,16,32,128]{3,2,1,0:T(8,128)(2,1)S(1)}, u32[]{:S(2)}, u32[]{:S(2)}) async-start(bf16[16,16,32,128]{3,2,1,0:T(8,128)(2,1)} %broadcast_select_fusion.1), calls=%async_computation.2 | async-start | bytes 4194304 | tf_op jit(solution)/shard_map/all_to_all | solution.py:225
  224.7 162.6 %all-reduce.5.cloned.1.call-start = ((), (), s32[]{:S(2)}) async-start(), calls=%async_computation.4 | async-start | bytes 1572864 | tf_op jit(solution)/shard_map/psum | solution.py:257
  392.9 4.8 copy-start.13
Sparse Core Ops, SparseCore 0:
  10.7 46.4 all-gather.2
  230.8 156.3 all-reduce.4
